TPU v7x, 32 devices: a whole 2x2x4 slice. The times are simulated.
32 devices in a mesh: pix: 16 (over z, y, core), frm: 2 (over x).
Axes of the slice: x: 2, y: 2, z: 4, core: 2. Of those that a mesh axis runs over, the one named last changes fastest.
Arguments:
- frames: bfloat16 [65536, 768], P('pix', 'frm'), may hold values from 0 to 6
- footprints: bfloat16 [65536, 192], P('pix'), may hold values from 0 to 0.024414062
- support: int32 [4096, 192], P('pix'), may hold values 0 or 1
- traces: float32 [1024, 768], P('pix', 'frm'), may hold values from 0 to 2
- block_order: int32 [16, 2], replicated, may hold values from 0 to 1, each once within a row
Outputs:
- refined: bfloat16 [65536, 192], P(('pix', 'frm'))
- updated: float32 [1024, 768], P('pix', 'frm')
Inputs may be any that keep to these rules, and one draw needn't show every extreme that they name: `block_order`: each row lists every block index of a slab once.
All inputs are finite; a program needn't handle non-finite values. No bound on the sum of `support` on one device may be relied on, other than what follows from the above.
Results may differ from a plain program's by a relative error of at most 0.0036.
Values may be sent and summed in bfloat16 or wider, within the bound.
A program may use at most 64 MiB of HBM per device.

v0:
```python
import jax
import jax.numpy as jnp
from jax import lax
from jax.sharding import PartitionSpec as P

BLOCK = 32
TILE = 16
highest = lax.Precision.HIGHEST


def from_behind(block, axis, distance):
    devices = range(lax.axis_size(axis))
    route = [(i - distance, i) for i in devices if i - distance in devices]
    return lax.ppermute(block, axis, route)


def window_mask(support, slab_id, owners, owner_width):
    expanded = jnp.repeat(support, TILE, axis=0).astype(jnp.float32)
    window_of = jnp.arange(3 * owner_width, dtype=jnp.int32) // owner_width
    usable = jnp.where(
        window_of == 0, slab_id > 0, jnp.where(window_of == 2, slab_id < owners - 1, True)
    )
    return expanded * usable.astype(jnp.float32)[None, :]


def trace_block(current, window, drive_rows, coupling, block_id, owner_width):
    row_start = block_id * BLOCK
    band_rows = lax.dynamic_slice_in_dim(coupling, row_start, BLOCK, 0)
    diagonal = jnp.diagonal(
        lax.dynamic_slice_in_dim(band_rows, 2 * owner_width + row_start, BLOCK, 1)
    )
    product = jnp.dot(band_rows, window, precision=highest)
    target = lax.dynamic_slice_in_dim(drive_rows, row_start, BLOCK, 0)
    before = lax.dynamic_slice_in_dim(current, row_start, BLOCK, 0)
    after = jnp.maximum(before + (target - product) / (diagonal[:, None] + 1.0), 0.0)
    return (after, row_start)


def trace_window(current):
    pieces = [from_behind(current, "pix", offset) for offset in (2, 1, -1, -2)]
    return jnp.concatenate([pieces[0], pieces[1], current, pieces[2], pieces[3]], axis=0)


def shards(frames, footprints, support, traces, block_order):
    owners = lax.axis_size("pix")
    slab_id = lax.axis_index("pix")
    owner_width = traces.shape[0]
    sweeps = owner_width // BLOCK
    keep = window_mask(support, slab_id, owners, owner_width)
    active = (footprints.astype(jnp.float32) * keep).astype(jnp.bfloat16)
    loads = jnp.einsum("pk,pt->kt", active, frames, preferred_element_type=jnp.float32)
    correlations = jnp.einsum("pk,pj->kj", active, active, preferred_element_type=jnp.float32)
    drive_rows = loads[owner_width : 2 * owner_width]
    coupling = jnp.pad(
        correlations[owner_width : 2 * owner_width], ((0, 0), (owner_width, owner_width))
    )
    for offset, window_id in ((-1, 0), (1, 2)):
        lower = window_id * owner_width
        arrived = from_behind(
            (loads[lower : lower + owner_width], correlations[lower : lower + owner_width]),
            "pix",
            offset,
        )
        drive_rows = drive_rows + arrived[0]
        if offset == -1:
            coupling = coupling + jnp.pad(arrived[1], ((0, 0), (2 * owner_width, 0)))
        else:
            coupling = coupling + jnp.pad(arrived[1], ((0, 0), (0, 2 * owner_width)))
    current = traces
    for step in range(sweeps):
        window = trace_window(current)
        after, row_start = trace_block(
            current, window, drive_rows, coupling, block_order[slab_id, step], owner_width
        )
        current = lax.dynamic_update_slice_in_dim(current, after, row_start, 0)
    beside = [from_behind(current, "pix", offset) for offset in (1, -1)]
    near_rows = jnp.concatenate([beside[0], current, beside[1]], axis=0)
    rounded = near_rows.astype(jnp.bfloat16)
    shares = lax.axis_size("frm")
    share_rows = footprints.shape[0] // shares
    row_begin = lax.axis_index("frm") * share_rows
    pixel_rows = lax.all_to_all(frames, "frm", split_axis=0, concat_axis=1, tiled=True)
    all_traces = lax.all_gather(rounded, "frm", axis=1, tiled=True)
    mixing = jnp.einsum("pt,kt->pk", pixel_rows, all_traces, preferred_element_type=jnp.float32)
    gram = jnp.einsum("kt,jt->kj", all_traces, all_traces, preferred_element_type=jnp.float32)
    shaped = lax.dynamic_slice_in_dim(active, row_begin, share_rows, 0).astype(jnp.float32)
    keep_rows = lax.dynamic_slice_in_dim(keep, row_begin, share_rows, 0)
    for step in range(sweeps):
        slab_near = jnp.clip(slab_id - 1 + jnp.arange(3, dtype=jnp.int32), 0, owners - 1)
        picked = block_order[slab_near, step]
        columns = (
            jnp.arange(3, dtype=jnp.int32)[:, None] * owner_width
            + picked[:, None] * BLOCK
            + jnp.arange(BLOCK, dtype=jnp.int32)[None, :]
        ).reshape(-1)
        gram_cols = jnp.take(gram, columns, axis=1)
        diagonal = jnp.diagonal(jnp.take(gram_cols, columns, axis=0))
        before = jnp.take(shaped, columns, axis=1)
        target = jnp.take(mixing, columns, axis=1)
        keep_cols = jnp.take(keep_rows, columns, axis=1)
        product = jnp.dot(shaped, gram_cols, precision=highest)
        after = (
            jnp.maximum(before + (target - product) / (diagonal[None, :] + 1.0), 0.0) * keep_cols
        )
        shaped = shaped.at[:, columns].set(after)
    return (shaped.astype(jnp.bfloat16), current)


def solution(mesh):
    in_specs = (P("pix", "frm"), P("pix", None), P("pix", None), P("pix", "frm"), P())
    out_specs = (P(("pix", "frm"), None), P("pix", "frm"))
    return jax.shard_map(shards, mesh=mesh, in_specs=in_specs, out_specs=out_specs, check_vma=False)
```

profile of v0, /device:TPU:10, one launch (start us, length us, event | category | flops | bytes accessed | tf_op | source)
XLA Modules:
  0.0 125.7 jit_solution(3920926233574790244)
XLA Ops:
  1.5 2.7 %collective-permute-start.6 = (f32[64,384]{1,0:T(8,128)S(1)}, f32[64,384]{1,0:T(8,128)}, u32[]{:S(2)}, u32[]{:S(2)}) collective-permute-start(f32[64,384]{1,0:T(8,128)S(1)} %copy.38), channel_id=1, source_target_pairs={{2,0},{4,2},{6,4},{8,6},{10,8},{12,10},{14,12},{16,14},{18,16},{20... | collective-permute-start | bytes 294920 | tf_op jit(solution)/shard_map/ppermute | solution.py:14
  4.3 1.9 %collective-permute-start.5 = (f32[64,384]{1,0:T(8,128)S(1)}, f32[64,384]{1,0:T(8,128)}, u32[]{:S(2)}, u32[]{:S(2)}) collective-permute-start(f32[64,384]{1,0:T(8,128)S(1)} %copy.38), channel_id=1, source_target_pairs={{0,2},{2,4},{4,6},{6,8},{8,10},{10,12},{12,14},{14,16},{16,18},{18... | collective-permute-start | bytes 294920 | tf_op jit(solution)/shard_map/ppermute | solution.py:14
  6.2 3.1 %collective-permute-start.4 = (f32[64,384]{1,0:T(8,128)S(1)}, f32[64,384]{1,0:T(8,128)}, u32[]{:S(2)}, u32[]{:S(2)}) collective-permute-start(f32[64,384]{1,0:T(8,128)S(1)} %copy.38), channel_id=1, source_target_pairs={{0,4},{2,6},{4,8},{6,10},{8,12},{10,14},{12,16},{14,18},{16,20},{1... | collective-permute-start | bytes 294920 | tf_op jit(solution)/shard_map/ppermute | solution.py:14
  9.3 5.9 %all-to-all-start = ((bf16[2,2048,384]{2,1,0:T(8,128)(2,1)}), bf16[2,2048,384]{2,1,0:T(8,128)(2,1)}, u32[]{:S(2)}, u32[]{:S(2)}) async-start(bf16[2,2048,384]{2,1,0:T(8,128)(2,1)} %bitcast.56), calls=%async_computation | async-start | bytes 6291456 | tf_op jit(solution)/shard_map/all_to_all | solution.py:82
  15.3 2.3 %broadcast_in_dim.69 = f32[256,16,192]{2,1,0:T(8,128)} broadcast(f32[256,192]{1,0:T(8,128)S(1)} %copy.17), dimensions={0,2} | broadcast | bytes 3342336 | tf_op jit(solution)/shard_map/broadcast_in_dim | solution.py:18
  17.6 5.4 %copy.18 = f32[4096,192]{0,1:T(8,128)} copy(f32[4096,192]{1,0:T(8,128)} %bitcast.55) | data formatting | bytes 6291456 | tf_op jit(solution)/shard_map/convert_element_type | solution.py:18
  23.1 4.4 %multiply_convert_fusion = (bf16[4096,192]{0,1:T(8,128)(2,1)S(1)}, f32[4096,192]{0,1:T(8,128)}) fusion(bf16[4096,192]{0,1:T(8,128)(2,1)S(1)} %copy-done.5, f32[4096,192]{0,1:T(8,128)} %copy.18, f32[192]{0:T(256)S(1)} %select_convert_fusion), kind=kLoop, calls=%fused_computation.18 | loop fusion | flops 3145728 | bytes 9437952 | tf_op jit(solution)/shard_map/convert_element_type | solution.py:50
  28.8 3.3 %collective-permute-start.3 = (f32[64,192]{1,0:T(8,128)}, f32[64,192]{1,0:T(8,128)}, u32[]{:S(2)}, u32[]{:S(2)}) collective-permute-start(f32[64,192]{1,0:T(8,128)} %get-tuple-element.10), channel_id=1, source_target_pairs={{0,2},{2,4},{4,6},{6,8},{8,10},{10,12},{12,14},{14,16},{16,18},{18... | collective-permute-start | bytes 147464 | tf_op jit(solution)/shard_map/ppermute | solution.py:14
  32.1 3.1 %collective-permute-start.2 = (f32[64,192]{1,0:T(8,128)}, f32[64,192]{1,0:T(8,128)}, u32[]{:S(2)}, u32[]{:S(2)}) collective-permute-start(f32[64,192]{1,0:T(8,128)} %get-tuple-element.11), channel_id=1, source_target_pairs={{2,0},{4,2},{6,4},{8,6},{10,8},{12,10},{14,12},{16,14},{18,16},{20... | collective-permute-start | bytes 147464 | tf_op jit(solution)/shard_map/ppermute | solution.py:14
  38.7 2.9 %fusion.32 = f32[192,384]{1,0:T(8,128)S(1)} fusion(bf16[4096,192]{0,1:T(8,128)(2,1)S(1)} %get-tuple-element.4, bf16[4096,384]{1,0:T(8,128)(2,1)} %param.11), kind=kOutput, calls=%fused_computation.100 | convolution fusion | flops 603979776 | bytes 5013504 | tf_op jit(solution)/shard_map/pk,pt->kt/dot_general | solution.py:51
  46.5 2.8 %collective-permute-start.7 = (f32[64,384]{1,0:T(8,128)S(1)}, f32[64,384]{1,0:T(8,128)S(1)}, u32[]{:S(2)}, u32[]{:S(2)}) collective-permute-start(f32[64,384]{1,0:T(8,128)S(1)} %copy.38), channel_id=1, source_target_pairs={{4,0},{6,2},{8,4},{10,6},{12,8},{14,10},{16,12},{18,14},{20,16},{2... | collective-permute-start | bytes 294920 | tf_op jit(solution)/shard_map/ppermute | solution.py:14
  49.4 2.7 %collective-permute-start = (f32[64,384]{1,0:T(8,128)}, f32[64,384]{1,0:T(8,128)}, u32[]{:S(2)}, u32[]{:S(2)}) collective-permute-start(f32[64,384]{1,0:T(8,128)} %get-tuple-element.7), channel_id=1, source_target_pairs={{2,0},{4,2},{6,4},{8,6},{10,8},{12,10},{14,12},{16,14},{18,16},{20... | collective-permute-start | bytes 294920 | tf_op jit(solution)/shard_map/ppermute | solution.py:14
  54.7 1.9 %collective-permute-start.1 = (f32[64,384]{1,0:T(8,128)}, f32[64,384]{1,0:T(8,128)S(1)}, u32[]{:S(2)}, u32[]{:S(2)}) collective-permute-start(f32[64,384]{1,0:T(8,128)} %get-tuple-element.8), channel_id=1, source_target_pairs={{0,2},{2,4},{4,6},{6,8},{8,10},{10,12},{12,14},{14,16},{16,18},{18... | collective-permute-start | bytes 294920 | tf_op jit(solution)/shard_map/ppermute | solution.py:14
  59.3 2.4 %collective-permute-done.1 = f32[64,384]{1,0:T(8,128)S(1)} collective-permute-done((f32[64,384]{1,0:T(8,128)}, f32[64,384]{1,0:T(8,128)S(1)}, u32[]{:S(2)}, u32[]{:S(2)}) %collective-permute-start.1) | collective-permute-done | bytes 98336 | tf_op jit(solution)/shard_map/ppermute | solution.py:14
  63.0 1.9 %collective-permute-start.8 = (f32[64,384]{1,0:T(8,128)S(1)}, f32[64,384]{1,0:T(8,128)S(1)}, u32[]{:S(2)}, u32[]{:S(2)}) collective-permute-start(f32[64,384]{1,0:T(8,128)S(1)} %maximum_dynamic-update-slice_fusion.1), channel_id=1, source_target_pairs={{0,4},{2,6},{4,8},{6,10},{8,12},{10,14},{12,16},{14,18},{16,20},{1... | collective-permute-start | bytes 294920 | tf_op jit(solution)/shard_map/ppermute | solution.py:14
  65.0 4.8 %collective-permute-start.11 = (f32[64,384]{1,0:T(8,128)S(1)}, f32[64,384]{1,0:T(8,128)S(1)}, u32[]{:S(2)}, u32[]{:S(2)}) collective-permute-start(f32[64,384]{1,0:T(8,128)S(1)} %maximum_dynamic-update-slice_fusion.1), channel_id=1, source_target_pairs={{4,0},{6,2},{8,4},{10,6},{12,8},{14,10},{16,12},{18,14},{20,16},{2... | collective-permute-start | bytes 294920 | tf_op jit(solution)/shard_map/ppermute | solution.py:14
  69.8 1.9 %collective-permute-start.10 = (f32[64,384]{1,0:T(8,128)S(1)}, f32[64,384]{1,0:T(8,128)S(1)}, u32[]{:S(2)}, u32[]{:S(2)}) collective-permute-start(f32[64,384]{1,0:T(8,128)S(1)} %maximum_dynamic-update-slice_fusion.1), channel_id=1, source_target_pairs={{2,0},{4,2},{6,4},{8,6},{10,8},{12,10},{14,12},{16,14},{18,16},{20... | collective-permute-start | bytes 294920 | tf_op jit(solution)/shard_map/ppermute | solution.py:14
  71.7 2.4 %collective-permute-start.9 = (f32[64,384]{1,0:T(8,128)S(1)}, f32[64,384]{1,0:T(8,128)S(1)}, u32[]{:S(2)}, u32[]{:S(2)}) collective-permute-start(f32[64,384]{1,0:T(8,128)S(1)} %maximum_dynamic-update-slice_fusion.1), channel_id=1, source_target_pairs={{0,2},{2,4},{4,6},{6,8},{8,10},{10,12},{12,14},{14,16},{16,18},{18... | collective-permute-start | bytes 294920 | tf_op jit(solution)/shard_map/ppermute | solution.py:14
  74.2 4.4 %collective-permute-done.9 = f32[64,384]{1,0:T(8,128)S(1)} collective-permute-done((f32[64,384]{1,0:T(8,128)S(1)}, f32[64,384]{1,0:T(8,128)S(1)}, u32[]{:S(2)}, u32[]{:S(2)}) %collective-permute-start.9) | collective-permute-done | bytes 98336 | tf_op jit(solution)/shard_map/ppermute | solution.py:14
  79.1 1.9 %collective-permute-start.13 = (bf16[64,384]{1,0:T(8,128)(2,1)S(1)}, bf16[64,384]{1,0:T(8,128)(2,1)S(1)}, u32[]{:S(2)}, u32[]{:S(2)}) collective-permute-start(bf16[64,384]{1,0:T(8,128)(2,1)S(1)} %convert.27), channel_id=1, source_target_pairs={{2,0},{4,2},{6,4},{8,6},{10,8},{12,10},{14,12},{16,14},{18,16},{20... | collective-permute-start | bytes 147464 | tf_op jit(solution)/shard_map/ppermute | solution.py:14
  81.0 2.4 %collective-permute-start.12 = (bf16[64,384]{1,0:T(8,128)(2,1)S(1)}, bf16[64,384]{1,0:T(8,128)(2,1)S(1)}, u32[]{:S(2)}, u32[]{:S(2)}) collective-permute-start(bf16[64,384]{1,0:T(8,128)(2,1)S(1)} %convert.27), channel_id=1, source_target_pairs={{0,2},{2,4},{4,6},{6,8},{8,10},{10,12},{12,14},{14,16},{16,18},{18... | collective-permute-start | bytes 147464 | tf_op jit(solution)/shard_map/ppermute | solution.py:14
  83.4 1.7 %gather_fusion.15 = f32[96,2048]{1,0:T(8,128)} fusion(f32[2048,192]{0,1:T(8,128)S(1)} %constant_dynamic-slice_fusion.1, s32[1024]{0:T(1024)S(1)} %get-tuple-element.23), kind=kCustom, calls=%fused_computation.7.clone | custom fusion | bytes 1573248 | tf_op jit(solution)/shard_map/jit(_take)/gather | solution.py:100
  86.9 1.8 %gather_fusion.6 = f32[96,2048]{1,0:T(8,128)} fusion(f32[2048,192]{0,1:T(8,128)S(1)} %dynamic-slice_convert_fusion, s32[1024]{0:T(1024)S(1)} %get-tuple-element.24), kind=kCustom, calls=%fused_computation.clone | custom fusion | bytes 1573248 | tf_op jit(solution)/shard_map/jit(_take)/gather | solution.py:98
  88.7 6.4 %all_gather.3 = bf16[192,768]{1,0:T(8,128)(2,1)S(1)} all-gather(bf16[192,384]{1,0:T(8,128)(2,1)S(1)} %pad_maximum_fusion), channel_id=1, replica_groups=mesh['pix'=16,'frm'=2] {'frm'}, dimensions={1}, use_global_device_ids=true | all-gather | bytes 442368 | tf_op jit(solution)/shard_map/all_gather | solution.py:83
  102.2 4.7 %copy.19 = bf16[2048,2,384]{0,2,1:T(8,128)(2,1)} copy(bf16[2048,2,384]{2,0,1:T(8,128)(2,1)} %bitcast.8) | data formatting | bytes 6291456 | tf_op jit(solution)/shard_map/all_to_all | solution.py:82
  106.9 2.7 %convolution_bitcast_fusion = f32[2048,192]{0,1:T(8,128)S(1)} fusion(bf16[192,768]{1,0:T(8,128)(2,1)S(1)} %all_gather.3, bf16[2048,768]{0,1:T(8,128)(2,1)} %bitcast.57), kind=kOutput, calls=%fused_computation.19 | convolution fusion | flops 603979776 | bytes 5013504 | tf_op jit(solution)/shard_map/pt,kt->pk/dot_general | solution.py:84
  109.6 1.8 %gather_fusion.12 = f32[96,2048]{1,0:T(8,128)} fusion(f32[2048,192]{0,1:T(8,128)S(1)} %convolution_bitcast_fusion, s32[1024]{0:T(1024)S(1)} %get-tuple-element.23), kind=kCustom, calls=%fused_computation.6.clone | custom fusion | bytes 1573248 | tf_op jit(solution)/shard_map/jit(_take)/gather | solution.py:99
  111.5 1.7 %gather_fusion.7 = f32[96,2048]{1,0:T(8,128)} fusion(f32[2048,192]{0,1:T(8,128)S(1)} %convolution_bitcast_fusion, s32[1024]{0:T(1024)S(1)} %get-tuple-element.24), kind=kCustom, calls=%fused_computation.3.clone | custom fusion | bytes 1573248 | tf_op jit(solution)/shard_map/jit(_take)/gather | solution.py:99
  113.2 2.5 %fusion.9 = f32[96,2048]{1,0:T(8,128)S(1)} fusion(f32[96,2048]{1,0:T(8,128)} %gather_fusion.10, f32[96,2048]{1,0:T(8,128)} %gather_fusion.7, f32[96,2048]{1,0:T(8,128)} %gather_fusion.6, bf16[4096,192]{0,1:T(8,128)(2,1)} %copy-done.1, s32[]{:T(128)S(6)} %select_n.126, f32[96]{0:T(128)S(1)} %copy-done.17, pred[96]{0:T(512)(128)(4,1)S(1)} %copy-done.11, ...), kind=kOutput, calls=%fused_computation.31 | convolution fusion | flops 454576128 | bytes 4032004 | tf_op jit(solution)/shard_map/dot_general | solution.py:101
  117.4 1.7 %gather_fusion.11 = f32[96,2048]{1,0:T(8,128)} fusion(f32[2048,192]{0,1:T(8,128)S(1)} %scatter_fusion, s32[1024]{0:T(1024)S(1)} %get-tuple-element.23), kind=kCustom, calls=%fused_computation.5.clone | custom fusion | bytes 1573248 | tf_op jit(solution)/shard_map/jit(_take)/gather | solution.py:98
  119.2 3.2 %fusion.5 = f32[96,2048]{1,0:T(8,128)} fusion(f32[2048,192]{0,1:T(8,128)S(1)} %scatter_fusion, f32[96,2048]{1,0:T(8,128)S(1)} %copy-done.2, f32[96,2048]{1,0:T(8,128)S(1)} %copy-done.3, f32[96,2048]{1,0:T(8,128)} %gather_fusion.11, f32[96]{0:T(128)S(1)} %copy-done.16, pred[96]{0:T(512)(128)(4,1)S(1)} %get-tuple-element.19, f32[96,192]{1,0:T(8,128)S(1)} %gather_fusion.13), kind=kOutput, calls=%fused_computation.27 | convolution fusion | flops 454576128 | bytes 4792800 | tf_op jit(solution)/shard_map/dot_general | solution.py:101
  122.4 2.2 %scatter_fusion.1 = f32[2048,192]{0,1:T(8,128)S(1)} fusion(f32[2048,192]{0,1:T(8,128)S(1)} %scatter_fusion, s32[96]{0:T(128)S(1)} %copy-done.12, f32[96,2048]{1,0:T(8,128)} %fusion.5), kind=kCustom, calls=%fused_computation.17 | custom fusion | bytes 2359680 | tf_op jit(solution)/shard_map/scatter | solution.py:105
  (117 shorter events, 27.9 us)
Async XLA Ops:
  1.5 56.9 %collective-permute-start.6 = (f32[64,384]{1,0:T(8,128)S(1)}, f32[64,384]{1,0:T(8,128)}, u32[]{:S(2)}, u32[]{:S(2)}) collective-permute-start(f32[64,384]{1,0:T(8,128)S(1)} %copy.38), channel_id=1, source_target_pairs={{2,0},{4,2},{6,4},{8,6},{10,8},{12,10},{14,12},{16,14},{18,16},{20... | collective-permute-start | bytes 294920 | tf_op jit(solution)/shard_map/ppermute | solution.py:14
  4.3 53.2 %collective-permute-start.5 = (f32[64,384]{1,0:T(8,128)S(1)}, f32[64,384]{1,0:T(8,128)}, u32[]{:S(2)}, u32[]{:S(2)}) collective-permute-start(f32[64,384]{1,0:T(8,128)S(1)} %copy.38), channel_id=1, source_target_pairs={{0,2},{2,4},{4,6},{6,8},{8,10},{10,12},{12,14},{14,16},{16,18},{18... | collective-permute-start | bytes 294920 | tf_op jit(solution)/shard_map/ppermute | solution.py:14
  6.2 48.5 %collective-permute-start.4 = (f32[64,384]{1,0:T(8,128)S(1)}, f32[64,384]{1,0:T(8,128)}, u32[]{:S(2)}, u32[]{:S(2)}) collective-permute-start(f32[64,384]{1,0:T(8,128)S(1)} %copy.38), channel_id=1, source_target_pairs={{0,4},{2,6},{4,8},{6,10},{8,12},{10,14},{12,16},{14,18},{16,20},{1... | collective-permute-start | bytes 294920 | tf_op jit(solution)/shard_map/ppermute | solution.py:14
  9.3 5.9 %copy-start.9 = (s32[256,192]{0,1:T(8,128)S(1)}, s32[256,192]{0,1:T(8,128)}, u32[]{:S(2)}) copy-start(s32[256,192]{0,1:T(8,128)} %param.13) | copy-start | bytes 589828
  9.3 92.9 %all-to-all-start = ((bf16[2,2048,384]{2,1,0:T(8,128)(2,1)}), bf16[2,2048,384]{2,1,0:T(8,128)(2,1)}, u32[]{:S(2)}, u32[]{:S(2)}) async-start(bf16[2,2048,384]{2,1,0:T(8,128)(2,1)} %bitcast.56), calls=%async_computation | async-start | bytes 6291456 | tf_op jit(solution)/shard_map/all_to_all | solution.py:82
  17.6 5.5 %copy-start.5 = (bf16[4096,192]{0,1:T(8,128)(2,1)S(1)}, bf16[4096,192]{0,1:T(8,128)(2,1)}, u32[]{:S(2)}) copy-start(bf16[4096,192]{0,1:T(8,128)(2,1)} %param.12) | copy-start | bytes 4718596
  27.5 14.1 %copy-start.1 = (bf16[4096,192]{0,1:T(8,128)(2,1)}, bf16[4096,192]{0,1:T(8,128)(2,1)S(1)}, u32[]{:S(2)}) copy-start(bf16[4096,192]{0,1:T(8,128)(2,1)S(1)} %get-tuple-element.4) | copy-start | bytes 4718596
  27.5 7.8 %copy-start = (s32[16,2]{0,1:T(2,128)S(1)}, s32[16,2]{0,1:T(2,128)}, u32[]{:S(2)}) copy-start(s32[16,2]{0,1:T(2,128)} %param.15) | copy-start | bytes 388
  28.8 17.8 %collective-permute-start.3 = (f32[64,192]{1,0:T(8,128)}, f32[64,192]{1,0:T(8,128)}, u32[]{:S(2)}, u32[]{:S(2)}) collective-permute-start(f32[64,192]{1,0:T(8,128)} %get-tuple-element.10), channel_id=1, source_target_pairs={{0,2},{2,4},{4,6},{6,8},{8,10},{10,12},{12,14},{14,16},{16,18},{18... | collective-permute-start | bytes 147464 | tf_op jit(solution)/shard_map/ppermute | solution.py:14
  32.1 17.3 %collective-permute-start.2 = (f32[64,192]{1,0:T(8,128)}, f32[64,192]{1,0:T(8,128)}, u32[]{:S(2)}, u32[]{:S(2)}) collective-permute-start(f32[64,192]{1,0:T(8,128)} %get-tuple-element.11), channel_id=1, source_target_pairs={{2,0},{4,2},{6,4},{8,6},{10,8},{12,10},{14,12},{16,14},{18,16},{20... | collective-permute-start | bytes 147464 | tf_op jit(solution)/shard_map/ppermute | solution.py:14
  41.6 1.7 %copy-start.6 = (f32[192,384]{1,0:T(8,128)}, f32[192,384]{1,0:T(8,128)S(1)}, u32[]{:S(2)}) copy-start(f32[192,384]{1,0:T(8,128)S(1)} %fusion.32) | copy-start | bytes 884740
  41.8 2.8 %copy-start.14 = (s32[96]{0:T(128)S(1)}, s32[96]{0:T(128)}, u32[]{:S(2)}) copy-start(s32[96]{0:T(128)} %compare_select_fusion) | copy-start | bytes 1156
  41.8 2.8 %copy-start.15 = (s32[96]{0:T(128)S(1)}, s32[96]{0:T(128)}, u32[]{:S(2)}) copy-start(s32[96]{0:T(128)} %compare_select_fusion.1) | copy-start | bytes 1156
  46.5 12.8 %collective-permute-start.7 = (f32[64,384]{1,0:T(8,128)S(1)}, f32[64,384]{1,0:T(8,128)S(1)}, u32[]{:S(2)}, u32[]{:S(2)}) collective-permute-start(f32[64,384]{1,0:T(8,128)S(1)} %copy.38), channel_id=1, source_target_pairs={{4,0},{6,2},{8,4},{10,6},{12,8},{14,10},{16,12},{18,14},{20,16},{2... | collective-permute-start | bytes 294920 | tf_op jit(solution)/shard_map/ppermute | solution.py:14
  49.4 10.0 %collective-permute-start = (f32[64,384]{1,0:T(8,128)}, f32[64,384]{1,0:T(8,128)}, u32[]{:S(2)}, u32[]{:S(2)}) collective-permute-start(f32[64,384]{1,0:T(8,128)} %get-tuple-element.7), channel_id=1, source_target_pairs={{2,0},{4,2},{6,4},{8,6},{10,8},{12,10},{14,12},{16,14},{18,16},{20... | collective-permute-start | bytes 294920 | tf_op jit(solution)/shard_map/ppermute | solution.py:14
  54.7 7.0 %collective-permute-start.1 = (f32[64,384]{1,0:T(8,128)}, f32[64,384]{1,0:T(8,128)S(1)}, u32[]{:S(2)}, u32[]{:S(2)}) collective-permute-start(f32[64,384]{1,0:T(8,128)} %get-tuple-element.8), channel_id=1, source_target_pairs={{0,2},{2,4},{4,6},{6,8},{8,10},{10,12},{12,14},{14,16},{16,18},{18... | collective-permute-start | bytes 294920 | tf_op jit(solution)/shard_map/ppermute | solution.py:14
  63.0 11.1 %collective-permute-start.8 = (f32[64,384]{1,0:T(8,128)S(1)}, f32[64,384]{1,0:T(8,128)S(1)}, u32[]{:S(2)}, u32[]{:S(2)}) collective-permute-start(f32[64,384]{1,0:T(8,128)S(1)} %maximum_dynamic-update-slice_fusion.1), channel_id=1, source_target_pairs={{0,4},{2,6},{4,8},{6,10},{8,12},{10,14},{12,16},{14,18},{16,20},{1... | collective-permute-start | bytes 294920 | tf_op jit(solution)/shard_map/ppermute | solution.py:14
  65.0 13.7 %collective-permute-start.11 = (f32[64,384]{1,0:T(8,128)S(1)}, f32[64,384]{1,0:T(8,128)S(1)}, u32[]{:S(2)}, u32[]{:S(2)}) collective-permute-start(f32[64,384]{1,0:T(8,128)S(1)} %maximum_dynamic-update-slice_fusion.1), channel_id=1, source_target_pairs={{4,0},{6,2},{8,4},{10,6},{12,8},{14,10},{16,12},{18,14},{20,16},{2... | collective-permute-start | bytes 294920 | tf_op jit(solution)/shard_map/ppermute | solution.py:14
  69.8 8.8 %collective-permute-start.10 = (f32[64,384]{1,0:T(8,128)S(1)}, f32[64,384]{1,0:T(8,128)S(1)}, u32[]{:S(2)}, u32[]{:S(2)}) collective-permute-start(f32[64,384]{1,0:T(8,128)S(1)} %maximum_dynamic-update-slice_fusion.1), channel_id=1, source_target_pairs={{2,0},{4,2},{6,4},{8,6},{10,8},{12,10},{14,12},{16,14},{18,16},{20... | collective-permute-start | bytes 294920 | tf_op jit(solution)/shard_map/ppermute | solution.py:14
  71.7 6.8 %collective-permute-start.9 = (f32[64,384]{1,0:T(8,128)S(1)}, f32[64,384]{1,0:T(8,128)S(1)}, u32[]{:S(2)}, u32[]{:S(2)}) collective-permute-start(f32[64,384]{1,0:T(8,128)S(1)} %maximum_dynamic-update-slice_fusion.1), channel_id=1, source_target_pairs={{0,2},{2,4},{4,6},{6,8},{8,10},{10,12},{12,14},{14,16},{16,18},{18... | collective-permute-start | bytes 294920 | tf_op jit(solution)/shard_map/ppermute | solution.py:14
  79.1 6.1 %copy-start.4 = (f32[64,384]{1,0:T(8,128)}, f32[64,384]{1,0:T(8,128)S(1)}, u32[]{:S(2)}) copy-start(f32[64,384]{1,0:T(8,128)S(1)} %maximum_dynamic-update-slice_fusion) | copy-start | bytes 294916
  79.1 9.6 %collective-permute-start.13 = (bf16[64,384]{1,0:T(8,128)(2,1)S(1)}, bf16[64,384]{1,0:T(8,128)(2,1)S(1)}, u32[]{:S(2)}, u32[]{:S(2)}) collective-permute-start(bf16[64,384]{1,0:T(8,128)(2,1)S(1)} %convert.27), channel_id=1, source_target_pairs={{2,0},{4,2},{6,4},{8,6},{10,8},{12,10},{14,12},{16,14},{18,16},{20... | collective-permute-start | bytes 147464 | tf_op jit(solution)/shard_map/ppermute | solution.py:14
  81.0 7.7 %collective-permute-start.12 = (bf16[64,384]{1,0:T(8,128)(2,1)S(1)}, bf16[64,384]{1,0:T(8,128)(2,1)S(1)}, u32[]{:S(2)}, u32[]{:S(2)}) collective-permute-start(bf16[64,384]{1,0:T(8,128)(2,1)S(1)} %convert.27), channel_id=1, source_target_pairs={{0,2},{2,4},{4,6},{6,8},{8,10},{10,12},{12,14},{14,16},{16,18},{18... | collective-permute-start | bytes 147464 | tf_op jit(solution)/shard_map/ppermute | solution.py:14
  95.2 2.5 %copy-start.10 = (pred[96]{0:T(512)(128)(4,1)S(1)}, pred[96]{0:T(512)(128)(4,1)}, u32[]{:S(2)}) copy-start(pred[96]{0:T(512)(128)(4,1)} %get-tuple-element.20) | copy-start | bytes 292
  96.1 3.7 %copy-start.7 = (f32[96,192]{1,0:T(8,128)}, f32[96,192]{1,0:T(8,128)S(1)}, u32[]{:S(2)}) copy-start(f32[96,192]{1,0:T(8,128)S(1)} %gather_fusion.8) | copy-start | bytes 221188
  111.4 1.7 %copy-start.11 = (pred[96]{0:T(512)(128)(4,1)S(1)}, pred[96]{0:T(512)(128)(4,1)}, u32[]{:S(2)}) copy-start(pred[96]{0:T(512)(128)(4,1)} %get-tuple-element.20) | copy-start | bytes 292
  111.5 1.7 %copy-start.17 = (f32[96]{0:T(128)S(1)}, f32[96]{0:T(128)}, u32[]{:S(2)}) copy-start(f32[96]{0:T(128)} %broadcast_add_fusion.1) | copy-start | bytes 1156
  113.2 2.6 %copy-start.13 = (s32[96]{0:T(128)S(1)}, s32[96]{0:T(128)}, u32[]{:S(2)}) copy-start(s32[96]{0:T(128)} %get-tuple-element.21) | copy-start | bytes 1156
  117.4 1.8 %copy-start.2 = (f32[96,2048]{1,0:T(8,128)S(1)}, f32[96,2048]{1,0:T(8,128)}, u32[]{:S(2)}) copy-start(f32[96,2048]{1,0:T(8,128)} %gather_fusion.15) | copy-start | bytes 2359300
  117.4 1.8 %copy-start.3 = (f32[96,2048]{1,0:T(8,128)S(1)}, f32[96,2048]{1,0:T(8,128)}, u32[]{:S(2)}) copy-start(f32[96,2048]{1,0:T(8,128)} %gather_fusion.12) | copy-start | bytes 2359300
  117.4 1.7 %copy-start.16 = (f32[96]{0:T(128)S(1)}, f32[96]{0:T(128)}, u32[]{:S(2)}) copy-start(f32[96]{0:T(128)} %broadcast_add_fusion) | copy-start | bytes 1156
  119.2 3.2 %copy-start.12 = (s32[96]{0:T(128)S(1)}, s32[96]{0:T(128)}, u32[]{:S(2)}) copy-start(s32[96]{0:T(128)} %get-tuple-element.22) | copy-start | bytes 1156
  (1 other events, 1.7 us)
where the time goes:
time: 127 us; the launch traced here: 126 us
  starting transfers between devices  42.9 us (34%)
  local copies, waits for them, and re-layouts  42.8 us (34%)
  matrix products  12.9 us (10%)
  other arithmetic  11.3 us (9%)
  waiting for transfers between devices  6.78 us (5%)
  blocking collectives  6.44 us (5%)
  between operations  2.49 us (2%)
    ppermute x14, starting transfers between devices, from_behind(): return lax.ppermute(block, axis, route)  37.1 us
    ppermute x14, waiting for transfers between devices, from_behind(): return lax.ppermute(block, axis, route)  6.78 us
    all_gather x1, blocking collectives, shards(): all_traces = lax.all_gather(rounded, 'frm', axis=1, tiled=True)  6.44 us
    all_to_all x1, starting transfers between devices, shards(): lax.all_to_all(frames, 'frm', split_axis=0, concat_axis=1, tiled=True)  5.87 us
    dot_general x2, matrix products, shards(): product = jnp.dot(shaped, gram_cols, precision=highest)  5.75 us
    convert_element_type x2, local copies, waits for them, and re-layouts, window_mask(): expanded = jnp.repeat(support, TILE, axis=0).astype(jnp.float32)  5.58 us
    all_to_all x1, local copies, waits for them, and re-layouts, shards(): lax.all_to_all(frames, 'frm', split_axis=0, concat_axis=1, tiled=True)  4.7 us
    convert_element_type x1, other arithmetic, shards(): active = (footprints.astype(jnp.float32) * keep).astype(jnp.bfloat16)  4.39 us
  transfers between devices with their start and end apart: 15, of which 2 were waited for; matrix products, arithmetic and copies ran while one was open for 34% of the time, Pallas kernels for 0%

commit v1 on v0

--- a/solution.py
+++ b/solution.py
@@ -79,7 +79,10 @@
     shares = lax.axis_size("frm")
     share_rows = footprints.shape[0] // shares
     row_begin = lax.axis_index("frm") * share_rows
-    pixel_rows = lax.all_to_all(frames, "frm", split_axis=0, concat_axis=1, tiled=True)
+    pixel_rows = jnp.concatenate(
+        lax.all_to_all(jnp.stack(jnp.split(frames, lax.axis_size("frm"), axis=0)), "frm", 0, 0),
+        axis=1,
+    )
     all_traces = lax.all_gather(rounded, "frm", axis=1, tiled=True)
     mixing = jnp.einsum("pt,kt->pk", pixel_rows, all_traces, preferred_element_type=jnp.float32)
     gram = jnp.einsum("kt,jt->kj", all_traces, all_traces, preferred_element_type=jnp.float32)

time: 127 us -> 132 us (1.039)
  other arithmetic: 11.3 us -> 14.8 us
  local copies, waits for them, and re-layouts: 42.8 us -> 44.8 us
    all_to_all x1 -> x0, local copies, waits for them, and re-layouts: 4.7 us -> none  [shards(): lax.all_to_all(frames, 'frm', split_axis=0, concat_axis=1, tiled=True)]
    split x0 -> x1, local copies, waits for them, and re-layouts: none -> 3.39 us  [shards(): jnp.split(frames, lax.axis_size('frm'), axis=0)]
    unnamed x45 -> x47, local copies, waits for them, and re-layouts: 3.72 us -> 7.08 us
    another operation x0 -> x1, other arithmetic: none -> 3.34 us  [shards(): jnp.stack(jnp.split(frames, lax.axis_size('frm'), axis=0))]
  transfers between devices with their start and end apart: 15 -> 15, of which waited for: 2 -> 2; matrix products, arithmetic and copies ran while one was open for 34% -> 40% of each run, Pallas kernels for 0% -> 0%
where the time goes in v1:
time: 132 us; the launch traced here: 131 us
  local copies, waits for them, and re-layouts  44.8 us (34%)
  starting transfers between devices  43 us (33%)
  other arithmetic  14.8 us (11%)
  matrix products  12.9 us (10%)
  waiting for transfers between devices  6.78 us (5%)
  blocking collectives  6.44 us (5%)
  between operations  2.57 us (2%)
    ppermute x14, starting transfers between devices, from_behind(): return lax.ppermute(block, axis, route)  37.1 us
    unnamed x47, local copies, waits for them, and re-layouts  7.08 us
    ppermute x14, waiting for transfers between devices, from_behind(): return lax.ppermute(block, axis, route)  6.78 us
    all_gather x1, blocking collectives, shards(): all_traces = lax.all_gather(rounded, 'frm', axis=1, tiled=True)  6.44 us
    all_to_all x1, starting transfers between devices, shards(): lax.all_to_all(jnp.stack(jnp.split(frames, lax.axis_size('frm'), axis=0))...  5.93 us
    dot_general x2, matrix products, shards(): product = jnp.dot(shaped, gram_cols, precision=highest)  5.74 us
    convert_element_type x2, local copies, waits for them, and re-layouts, window_mask(): expanded = jnp.repeat(support, TILE, axis=0).astype(jnp.float32)  5.51 us
    convert_element_type x1, other arithmetic, shards(): active = (footprints.astype(jnp.float32) * keep).astype(jnp.bfloat16)  4.37 us
  transfers between devices with their start and end apart: 15, of which 2 were waited for; matrix products, arithmetic and copies ran while one was open for 40% of the time, Pallas kernels for 0%

profile of v1, /device:TPU:10, one launch (start us, length us, event | category | flops | bytes accessed | tf_op | source)
XLA Modules:
  0.0 131.2 jit_solution(2409614321807944653)
XLA Ops:
  1.5 2.7 %collective-permute-start.6 = (f32[64,384]{1,0:T(8,128)S(1)}, f32[64,384]{1,0:T(8,128)}, u32[]{:S(2)}, u32[]{:S(2)}) collective-permute-start(f32[64,384]{1,0:T(8,128)S(1)} %copy.35), channel_id=1, source_target_pairs={{2,0},{4,2},{6,4},{8,6},{10,8},{12,10},{14,12},{16,14},{18,16},{20... | collective-permute-start | bytes 294920 | tf_op jit(solution)/shard_map/ppermute | solution.py:14
  4.3 1.9 %collective-permute-start.5 = (f32[64,384]{1,0:T(8,128)S(1)}, f32[64,384]{1,0:T(8,128)}, u32[]{:S(2)}, u32[]{:S(2)}) collective-permute-start(f32[64,384]{1,0:T(8,128)S(1)} %copy.35), channel_id=1, source_target_pairs={{0,2},{2,4},{4,6},{6,8},{8,10},{10,12},{12,14},{14,16},{16,18},{18... | collective-permute-start | bytes 294920 | tf_op jit(solution)/shard_map/ppermute | solution.py:14
  6.2 3.1 %collective-permute-start.4 = (f32[64,384]{1,0:T(8,128)S(1)}, f32[64,384]{1,0:T(8,128)}, u32[]{:S(2)}, u32[]{:S(2)}) collective-permute-start(f32[64,384]{1,0:T(8,128)S(1)} %copy.35), channel_id=1, source_target_pairs={{0,4},{2,6},{4,8},{6,10},{8,12},{10,14},{12,16},{14,18},{16,20},{1... | collective-permute-start | bytes 294920 | tf_op jit(solution)/shard_map/ppermute | solution.py:14
  9.3 3.4 %fusion.28 = (bf16[2048,384]{1,0:T(8,128)(2,1)}, bf16[2048,384]{1,0:T(8,128)(2,1)S(1)}) fusion(bf16[4096,384]{1,0:T(8,128)(2,1)} %param.11), kind=kLoop, calls=%fused_computation.96 | loop fusion | bytes 6291456 | tf_op jit(solution)/shard_map/split | solution.py:83
  16.1 3.3 %pad_maximum_fusion = bf16[2,2048,384]{1,2,0:T(8,128)(2,1)} fusion(bf16[1,2048,384]{1,2,0:T(8,128)(2,1)} %bitcast.57, bf16[1,2048,384]{1,2,0:T(8,128)(2,1)S(1)} %bitcast.56), kind=kLoop, calls=%fused_computation.18 | loop fusion | flops 1572864 | bytes 6291456 | tf_op jit(solution)/shard_map/stack | solution.py:83
  19.4 5.9 %all-to-all-start = ((bf16[2,2048,384]{1,2,0:T(8,128)(2,1)}), bf16[2,2048,384]{1,2,0:T(8,128)(2,1)}, u32[]{:S(2)}, u32[]{:S(2)}) async-start(bf16[2,2048,384]{1,2,0:T(8,128)(2,1)} %pad_maximum_fusion), calls=%async_computation | async-start | bytes 6291456 | tf_op jit(solution)/shard_map/all_to_all | solution.py:83
  25.5 2.3 %broadcast_in_dim.69 = f32[256,16,192]{2,1,0:T(8,128)} broadcast(f32[256,192]{1,0:T(8,128)S(1)} %copy.11), dimensions={0,2} | broadcast | bytes 3342336 | tf_op jit(solution)/shard_map/broadcast_in_dim | solution.py:18
  27.8 5.4 %copy.12 = f32[4096,192]{0,1:T(8,128)} copy(f32[4096,192]{1,0:T(8,128)} %bitcast.55) | data formatting | bytes 6291456 | tf_op jit(solution)/shard_map/convert_element_type | solution.py:18
  33.2 4.4 %multiply_convert_fusion = (bf16[4096,192]{0,1:T(8,128)(2,1)S(1)}, f32[4096,192]{0,1:T(8,128)}) fusion(bf16[4096,192]{0,1:T(8,128)(2,1)S(1)} %copy-done.5, f32[4096,192]{0,1:T(8,128)} %copy.12, f32[192]{0:T(256)S(1)} %select_convert_fusion), kind=kLoop, calls=%fused_computation.19 | loop fusion | flops 3145728 | bytes 9437952 | tf_op jit(solution)/shard_map/convert_element_type | solution.py:50
  38.8 3.3 %collective-permute-start.3 = (f32[64,192]{1,0:T(8,128)}, f32[64,192]{1,0:T(8,128)}, u32[]{:S(2)}, u32[]{:S(2)}) collective-permute-start(f32[64,192]{1,0:T(8,128)} %get-tuple-element.12), channel_id=1, source_target_pairs={{0,2},{2,4},{4,6},{6,8},{8,10},{10,12},{12,14},{14,16},{16,18},{18... | collective-permute-start | bytes 147464 | tf_op jit(solution)/shard_map/ppermute | solution.py:14
  42.2 3.1 %collective-permute-start.2 = (f32[64,192]{1,0:T(8,128)}, f32[64,192]{1,0:T(8,128)}, u32[]{:S(2)}, u32[]{:S(2)}) collective-permute-start(f32[64,192]{1,0:T(8,128)} %get-tuple-element.13), channel_id=1, source_target_pairs={{2,0},{4,2},{6,4},{8,6},{10,8},{12,10},{14,12},{16,14},{18,16},{20... | collective-permute-start | bytes 147464 | tf_op jit(solution)/shard_map/ppermute | solution.py:14
  48.8 2.9 %fusion.33 = f32[192,384]{1,0:T(8,128)S(1)} fusion(bf16[4096,192]{0,1:T(8,128)(2,1)S(1)} %get-tuple-element.4, bf16[4096,384]{1,0:T(8,128)(2,1)} %param.11), kind=kOutput, calls=%fused_computation.101 | convolution fusion | flops 603979776 | bytes 5013504 | tf_op jit(solution)/shard_map/pk,pt->kt/dot_general | solution.py:51
  56.8 2.8 %collective-permute-start.7 = (f32[64,384]{1,0:T(8,128)S(1)}, f32[64,384]{1,0:T(8,128)S(1)}, u32[]{:S(2)}, u32[]{:S(2)}) collective-permute-start(f32[64,384]{1,0:T(8,128)S(1)} %copy.35), channel_id=1, source_target_pairs={{4,0},{6,2},{8,4},{10,6},{12,8},{14,10},{16,12},{18,14},{20,16},{2... | collective-permute-start | bytes 294920 | tf_op jit(solution)/shard_map/ppermute | solution.py:14
  59.6 2.7 %collective-permute-start = (f32[64,384]{1,0:T(8,128)}, f32[64,384]{1,0:T(8,128)}, u32[]{:S(2)}, u32[]{:S(2)}) collective-permute-start(f32[64,384]{1,0:T(8,128)} %get-tuple-element.9), channel_id=1, source_target_pairs={{2,0},{4,2},{6,4},{8,6},{10,8},{12,10},{14,12},{16,14},{18,16},{20... | collective-permute-start | bytes 294920 | tf_op jit(solution)/shard_map/ppermute | solution.py:14
  64.9 1.9 %collective-permute-start.1 = (f32[64,384]{1,0:T(8,128)}, f32[64,384]{1,0:T(8,128)S(1)}, u32[]{:S(2)}, u32[]{:S(2)}) collective-permute-start(f32[64,384]{1,0:T(8,128)} %get-tuple-element.10), channel_id=1, source_target_pairs={{0,2},{2,4},{4,6},{6,8},{8,10},{10,12},{12,14},{14,16},{16,18},{18... | collective-permute-start | bytes 294920 | tf_op jit(solution)/shard_map/ppermute | solution.py:14
  69.6 2.4 %collective-permute-done.1 = f32[64,384]{1,0:T(8,128)S(1)} collective-permute-done((f32[64,384]{1,0:T(8,128)}, f32[64,384]{1,0:T(8,128)S(1)}, u32[]{:S(2)}, u32[]{:S(2)}) %collective-permute-start.1) | collective-permute-done | bytes 98336 | tf_op jit(solution)/shard_map/ppermute | solution.py:14
  73.3 1.9 %collective-permute-start.8 = (f32[64,384]{1,0:T(8,128)S(1)}, f32[64,384]{1,0:T(8,128)S(1)}, u32[]{:S(2)}, u32[]{:S(2)}) collective-permute-start(f32[64,384]{1,0:T(8,128)S(1)} %maximum_dynamic-update-slice_fusion.1), channel_id=1, source_target_pairs={{0,4},{2,6},{4,8},{6,10},{8,12},{10,14},{12,16},{14,18},{16,20},{1... | collective-permute-start | bytes 294920 | tf_op jit(solution)/shard_map/ppermute | solution.py:14
  75.2 4.8 %collective-permute-start.11 = (f32[64,384]{1,0:T(8,128)S(1)}, f32[64,384]{1,0:T(8,128)S(1)}, u32[]{:S(2)}, u32[]{:S(2)}) collective-permute-start(f32[64,384]{1,0:T(8,128)S(1)} %maximum_dynamic-update-slice_fusion.1), channel_id=1, source_target_pairs={{4,0},{6,2},{8,4},{10,6},{12,8},{14,10},{16,12},{18,14},{20,16},{2... | collective-permute-start | bytes 294920 | tf_op jit(solution)/shard_map/ppermute | solution.py:14
  80.0 1.9 %collective-permute-start.10 = (f32[64,384]{1,0:T(8,128)S(1)}, f32[64,384]{1,0:T(8,128)S(1)}, u32[]{:S(2)}, u32[]{:S(2)}) collective-permute-start(f32[64,384]{1,0:T(8,128)S(1)} %maximum_dynamic-update-slice_fusion.1), channel_id=1, source_target_pairs={{2,0},{4,2},{6,4},{8,6},{10,8},{12,10},{14,12},{16,14},{18,16},{20... | collective-permute-start | bytes 294920 | tf_op jit(solution)/shard_map/ppermute | solution.py:14
  82.0 2.4 %collective-permute-start.9 = (f32[64,384]{1,0:T(8,128)S(1)}, f32[64,384]{1,0:T(8,128)S(1)}, u32[]{:S(2)}, u32[]{:S(2)}) collective-permute-start(f32[64,384]{1,0:T(8,128)S(1)} %maximum_dynamic-update-slice_fusion.1), channel_id=1, source_target_pairs={{0,2},{2,4},{4,6},{6,8},{8,10},{10,12},{12,14},{14,16},{16,18},{18... | collective-permute-start | bytes 294920 | tf_op jit(solution)/shard_map/ppermute | solution.py:14
  84.4 4.4 %collective-permute-done.9 = f32[64,384]{1,0:T(8,128)S(1)} collective-permute-done((f32[64,384]{1,0:T(8,128)S(1)}, f32[64,384]{1,0:T(8,128)S(1)}, u32[]{:S(2)}, u32[]{:S(2)}) %collective-permute-start.9) | collective-permute-done | bytes 98336 | tf_op jit(solution)/shard_map/ppermute | solution.py:14
  89.3 1.9 %collective-permute-start.13 = (bf16[64,384]{1,0:T(8,128)(2,1)S(1)}, bf16[64,384]{1,0:T(8,128)(2,1)S(1)}, u32[]{:S(2)}, u32[]{:S(2)}) collective-permute-start(bf16[64,384]{1,0:T(8,128)(2,1)S(1)} %convert.27), channel_id=1, source_target_pairs={{2,0},{4,2},{6,4},{8,6},{10,8},{12,10},{14,12},{16,14},{18,16},{20... | collective-permute-start | bytes 147464 | tf_op jit(solution)/shard_map/ppermute | solution.py:14
  91.2 2.4 %collective-permute-start.12 = (bf16[64,384]{1,0:T(8,128)(2,1)S(1)}, bf16[64,384]{1,0:T(8,128)(2,1)S(1)}, u32[]{:S(2)}, u32[]{:S(2)}) collective-permute-start(bf16[64,384]{1,0:T(8,128)(2,1)S(1)} %convert.27), channel_id=1, source_target_pairs={{0,2},{2,4},{4,6},{6,8},{8,10},{10,12},{12,14},{14,16},{16,18},{18... | collective-permute-start | bytes 147464 | tf_op jit(solution)/shard_map/ppermute | solution.py:14
  97.1 1.7 %gather_fusion.6 = f32[96,2048]{1,0:T(8,128)} fusion(f32[2048,192]{0,1:T(8,128)S(1)} %dynamic-slice_convert_fusion, s32[1024]{0:T(1024)S(1)} %get-tuple-element.26), kind=kCustom, calls=%fused_computation.clone | custom fusion | bytes 1573248 | tf_op jit(solution)/shard_map/jit(_take)/gather | solution.py:101
  98.9 6.4 %all_gather.3 = bf16[192,768]{1,0:T(8,128)(2,1)S(1)} all-gather(bf16[192,384]{1,0:T(8,128)(2,1)S(1)} %pad_maximum_fusion.1), channel_id=1, replica_groups=mesh['pix'=16,'frm'=2] {'frm'}, dimensions={1}, use_global_device_ids=true | all-gather | bytes 442368 | tf_op jit(solution)/shard_map/all_gather | solution.py:86
  112.4 2.7 %fusion.36 = f32[2048,192]{0,1:T(8,128)S(1)} fusion(bf16[192,768]{1,0:T(8,128)(2,1)S(1)} %all_gather.3, bf16[2048,768]{0,1:T(8,128)(2,1)} %bitcast.7), kind=kOutput, calls=%fused_computation.104 | convolution fusion | flops 603979776 | bytes 5013504 | tf_op jit(solution)/shard_map/pt,kt->pk/dot_general | solution.py:87
  115.1 1.7 %gather_fusion.12 = f32[96,2048]{1,0:T(8,128)} fusion(f32[2048,192]{0,1:T(8,128)S(1)} %fusion.36, s32[1024]{0:T(1024)S(1)} %get-tuple-element.25), kind=kCustom, calls=%fused_computation.6.clone | custom fusion | bytes 1573248 | tf_op jit(solution)/shard_map/jit(_take)/gather | solution.py:102
  118.6 2.5 %fusion.9 = f32[96,2048]{1,0:T(8,128)S(1)} fusion(f32[96,2048]{1,0:T(8,128)} %gather_fusion.10, f32[96,2048]{1,0:T(8,128)} %gather_fusion.7, f32[96,2048]{1,0:T(8,128)} %gather_fusion.6, bf16[4096,192]{0,1:T(8,128)(2,1)} %copy-done.1, s32[]{:T(128)S(6)} %select_n.126, f32[96]{0:T(128)S(1)} %copy-done.17, pred[96]{0:T(512)(128)(4,1)S(1)} %copy-done.11, ...), kind=kOutput, calls=%fused_computation.31 | convolution fusion | flops 454576128 | bytes 4032004 | tf_op jit(solution)/shard_map/dot_general | solution.py:104
  121.2 1.8 %scatter_fusion = f32[2048,192]{0,1:T(8,128)S(1)} fusion(f32[2048,192]{0,1:T(8,128)S(1)} %dynamic-slice_convert_fusion, s32[96]{0:T(128)S(1)} %copy-done.13, f32[96,2048]{1,0:T(8,128)S(1)} %fusion.9), kind=kCustom, calls=%fused_computation.16 | custom fusion | bytes 2359680 | tf_op jit(solution)/shard_map/scatter | solution.py:108
  123.0 1.7 %gather_fusion.11 = f32[96,2048]{1,0:T(8,128)} fusion(f32[2048,192]{0,1:T(8,128)S(1)} %scatter_fusion, s32[1024]{0:T(1024)S(1)} %get-tuple-element.25), kind=kCustom, calls=%fused_computation.5.clone | custom fusion | bytes 1573248 | tf_op jit(solution)/shard_map/jit(_take)/gather | solution.py:101
  124.8 3.2 %fusion.5 = f32[96,2048]{1,0:T(8,128)} fusion(f32[2048,192]{0,1:T(8,128)S(1)} %scatter_fusion, f32[96,2048]{1,0:T(8,128)S(1)} %copy-done.2, f32[96,2048]{1,0:T(8,128)S(1)} %copy-done.3, f32[96,2048]{1,0:T(8,128)} %gather_fusion.11, f32[96]{0:T(128)S(1)} %copy-done.16, pred[96]{0:T(512)(128)(4,1)S(1)} %get-tuple-element.21, f32[96,192]{1,0:T(8,128)S(1)} %gather_fusion.13), kind=kOutput, calls=%fused_computation.27 | convolution fusion | flops 454576128 | bytes 4792800 | tf_op jit(solution)/shard_map/dot_general | solution.py:104
  128.0 2.2 %scatter_fusion.1 = f32[2048,192]{0,1:T(8,128)S(1)} fusion(f32[2048,192]{0,1:T(8,128)S(1)} %scatter_fusion, s32[96]{0:T(128)S(1)} %copy-done.12, f32[96,2048]{1,0:T(8,128)} %fusion.5), kind=kCustom, calls=%fused_computation.17 | custom fusion | bytes 2359680 | tf_op jit(solution)/shard_map/scatter | solution.py:108
  (120 shorter events, 33.1 us)
Async XLA Ops:
  1.5 67.1 %collective-permute-start.6 = (f32[64,384]{1,0:T(8,128)S(1)}, f32[64,384]{1,0:T(8,128)}, u32[]{:S(2)}, u32[]{:S(2)}) collective-permute-start(f32[64,384]{1,0:T(8,128)S(1)} %copy.35), channel_id=1, source_target_pairs={{2,0},{4,2},{6,4},{8,6},{10,8},{12,10},{14,12},{16,14},{18,16},{20... | collective-permute-start | bytes 294920 | tf_op jit(solution)/shard_map/ppermute | solution.py:14
  4.3 63.4 %collective-permute-start.5 = (f32[64,384]{1,0:T(8,128)S(1)}, f32[64,384]{1,0:T(8,128)}, u32[]{:S(2)}, u32[]{:S(2)}) collective-permute-start(f32[64,384]{1,0:T(8,128)S(1)} %copy.35), channel_id=1, source_target_pairs={{0,2},{2,4},{4,6},{6,8},{8,10},{10,12},{12,14},{14,16},{16,18},{18... | collective-permute-start | bytes 294920 | tf_op jit(solution)/shard_map/ppermute | solution.py:14
  6.2 58.7 %collective-permute-start.4 = (f32[64,384]{1,0:T(8,128)S(1)}, f32[64,384]{1,0:T(8,128)}, u32[]{:S(2)}, u32[]{:S(2)}) collective-permute-start(f32[64,384]{1,0:T(8,128)S(1)} %copy.35), channel_id=1, source_target_pairs={{0,4},{2,6},{4,8},{6,10},{8,12},{10,14},{12,16},{14,18},{16,20},{1... | collective-permute-start | bytes 294920 | tf_op jit(solution)/shard_map/ppermute | solution.py:14
  19.4 5.9 %copy-start.9 = (s32[256,192]{0,1:T(8,128)S(1)}, s32[256,192]{0,1:T(8,128)}, u32[]{:S(2)}) copy-start(s32[256,192]{0,1:T(8,128)} %param.13) | copy-start | bytes 589828
  19.4 93.0 %all-to-all-start = ((bf16[2,2048,384]{1,2,0:T(8,128)(2,1)}), bf16[2,2048,384]{1,2,0:T(8,128)(2,1)}, u32[]{:S(2)}, u32[]{:S(2)}) async-start(bf16[2,2048,384]{1,2,0:T(8,128)(2,1)} %pad_maximum_fusion), calls=%async_computation | async-start | bytes 6291456 | tf_op jit(solution)/shard_map/all_to_all | solution.py:83
  27.8 5.4 %copy-start.5 = (bf16[4096,192]{0,1:T(8,128)(2,1)S(1)}, bf16[4096,192]{0,1:T(8,128)(2,1)}, u32[]{:S(2)}) copy-start(bf16[4096,192]{0,1:T(8,128)(2,1)} %param.12) | copy-start | bytes 4718596
  37.6 14.2 %copy-start.1 = (bf16[4096,192]{0,1:T(8,128)(2,1)}, bf16[4096,192]{0,1:T(8,128)(2,1)S(1)}, u32[]{:S(2)}) copy-start(bf16[4096,192]{0,1:T(8,128)(2,1)S(1)} %get-tuple-element.4) | copy-start | bytes 4718596
  37.6 7.8 %copy-start = (s32[16,2]{0,1:T(2,128)S(1)}, s32[16,2]{0,1:T(2,128)}, u32[]{:S(2)}) copy-start(s32[16,2]{0,1:T(2,128)} %param.15) | copy-start | bytes 388
  38.8 17.9 %collective-permute-start.3 = (f32[64,192]{1,0:T(8,128)}, f32[64,192]{1,0:T(8,128)}, u32[]{:S(2)}, u32[]{:S(2)}) collective-permute-start(f32[64,192]{1,0:T(8,128)} %get-tuple-element.12), channel_id=1, source_target_pairs={{0,2},{2,4},{4,6},{6,8},{8,10},{10,12},{12,14},{14,16},{16,18},{18... | collective-permute-start | bytes 147464 | tf_op jit(solution)/shard_map/ppermute | solution.py:14
  42.2 17.4 %collective-permute-start.2 = (f32[64,192]{1,0:T(8,128)}, f32[64,192]{1,0:T(8,128)}, u32[]{:S(2)}, u32[]{:S(2)}) collective-permute-start(f32[64,192]{1,0:T(8,128)} %get-tuple-element.13), channel_id=1, source_target_pairs={{2,0},{4,2},{6,4},{8,6},{10,8},{12,10},{14,12},{16,14},{18,16},{20... | collective-permute-start | bytes 147464 | tf_op jit(solution)/shard_map/ppermute | solution.py:14
  51.7 1.7 %copy-start.6 = (f32[192,384]{1,0:T(8,128)}, f32[192,384]{1,0:T(8,128)S(1)}, u32[]{:S(2)}) copy-start(f32[192,384]{1,0:T(8,128)S(1)} %fusion.33) | copy-start | bytes 884740
  51.9 2.8 %copy-start.14 = (s32[96]{0:T(128)S(1)}, s32[96]{0:T(128)}, u32[]{:S(2)}) copy-start(s32[96]{0:T(128)} %compare_select_fusion) | copy-start | bytes 1156
  51.9 2.8 %copy-start.15 = (s32[96]{0:T(128)S(1)}, s32[96]{0:T(128)}, u32[]{:S(2)}) copy-start(s32[96]{0:T(128)} %compare_select_fusion.1) | copy-start | bytes 1156
  56.8 12.8 %collective-permute-start.7 = (f32[64,384]{1,0:T(8,128)S(1)}, f32[64,384]{1,0:T(8,128)S(1)}, u32[]{:S(2)}, u32[]{:S(2)}) collective-permute-start(f32[64,384]{1,0:T(8,128)S(1)} %copy.35), channel_id=1, source_target_pairs={{4,0},{6,2},{8,4},{10,6},{12,8},{14,10},{16,12},{18,14},{20,16},{2... | collective-permute-start | bytes 294920 | tf_op jit(solution)/shard_map/ppermute | solution.py:14
  59.6 9.9 %collective-permute-start = (f32[64,384]{1,0:T(8,128)}, f32[64,384]{1,0:T(8,128)}, u32[]{:S(2)}, u32[]{:S(2)}) collective-permute-start(f32[64,384]{1,0:T(8,128)} %get-tuple-element.9), channel_id=1, source_target_pairs={{2,0},{4,2},{6,4},{8,6},{10,8},{12,10},{14,12},{16,14},{18,16},{20... | collective-permute-start | bytes 294920 | tf_op jit(solution)/shard_map/ppermute | solution.py:14
  64.9 7.0 %collective-permute-start.1 = (f32[64,384]{1,0:T(8,128)}, f32[64,384]{1,0:T(8,128)S(1)}, u32[]{:S(2)}, u32[]{:S(2)}) collective-permute-start(f32[64,384]{1,0:T(8,128)} %get-tuple-element.10), channel_id=1, source_target_pairs={{0,2},{2,4},{4,6},{6,8},{8,10},{10,12},{12,14},{14,16},{16,18},{18... | collective-permute-start | bytes 294920 | tf_op jit(solution)/shard_map/ppermute | solution.py:14
  73.3 11.1 %collective-permute-start.8 = (f32[64,384]{1,0:T(8,128)S(1)}, f32[64,384]{1,0:T(8,128)S(1)}, u32[]{:S(2)}, u32[]{:S(2)}) collective-permute-start(f32[64,384]{1,0:T(8,128)S(1)} %maximum_dynamic-update-slice_fusion.1), channel_id=1, source_target_pairs={{0,4},{2,6},{4,8},{6,10},{8,12},{10,14},{12,16},{14,18},{16,20},{1... | collective-permute-start | bytes 294920 | tf_op jit(solution)/shard_map/ppermute | solution.py:14
  75.2 13.7 %collective-permute-start.11 = (f32[64,384]{1,0:T(8,128)S(1)}, f32[64,384]{1,0:T(8,128)S(1)}, u32[]{:S(2)}, u32[]{:S(2)}) collective-permute-start(f32[64,384]{1,0:T(8,128)S(1)} %maximum_dynamic-update-slice_fusion.1), channel_id=1, source_target_pairs={{4,0},{6,2},{8,4},{10,6},{12,8},{14,10},{16,12},{18,14},{20,16},{2... | collective-permute-start | bytes 294920 | tf_op jit(solution)/shard_map/ppermute | solution.py:14
  80.0 8.8 %collective-permute-start.10 = (f32[64,384]{1,0:T(8,128)S(1)}, f32[64,384]{1,0:T(8,128)S(1)}, u32[]{:S(2)}, u32[]{:S(2)}) collective-permute-start(f32[64,384]{1,0:T(8,128)S(1)} %maximum_dynamic-update-slice_fusion.1), channel_id=1, source_target_pairs={{2,0},{4,2},{6,4},{8,6},{10,8},{12,10},{14,12},{16,14},{18,16},{20... | collective-permute-start | bytes 294920 | tf_op jit(solution)/shard_map/ppermute | solution.py:14
  82.0 6.8 %collective-permute-start.9 = (f32[64,384]{1,0:T(8,128)S(1)}, f32[64,384]{1,0:T(8,128)S(1)}, u32[]{:S(2)}, u32[]{:S(2)}) collective-permute-start(f32[64,384]{1,0:T(8,128)S(1)} %maximum_dynamic-update-slice_fusion.1), channel_id=1, source_target_pairs={{0,2},{2,4},{4,6},{6,8},{8,10},{10,12},{12,14},{14,16},{16,18},{18... | collective-permute-start | bytes 294920 | tf_op jit(solution)/shard_map/ppermute | solution.py:14
  89.3 6.1 %copy-start.4 = (f32[64,384]{1,0:T(8,128)}, f32[64,384]{1,0:T(8,128)S(1)}, u32[]{:S(2)}) copy-start(f32[64,384]{1,0:T(8,128)S(1)} %maximum_dynamic-update-slice_fusion) | copy-start | bytes 294916
  89.3 9.5 %collective-permute-start.13 = (bf16[64,384]{1,0:T(8,128)(2,1)S(1)}, bf16[64,384]{1,0:T(8,128)(2,1)S(1)}, u32[]{:S(2)}, u32[]{:S(2)}) collective-permute-start(bf16[64,384]{1,0:T(8,128)(2,1)S(1)} %convert.27), channel_id=1, source_target_pairs={{2,0},{4,2},{6,4},{8,6},{10,8},{12,10},{14,12},{16,14},{18,16},{20... | collective-permute-start | bytes 147464 | tf_op jit(solution)/shard_map/ppermute | solution.py:14
  91.2 7.6 %collective-permute-start.12 = (bf16[64,384]{1,0:T(8,128)(2,1)S(1)}, bf16[64,384]{1,0:T(8,128)(2,1)S(1)}, u32[]{:S(2)}, u32[]{:S(2)}) collective-permute-start(bf16[64,384]{1,0:T(8,128)(2,1)S(1)} %convert.27), channel_id=1, source_target_pairs={{0,2},{2,4},{4,6},{6,8},{8,10},{10,12},{12,14},{14,16},{16,18},{18... | collective-permute-start | bytes 147464 | tf_op jit(solution)/shard_map/ppermute | solution.py:14
  105.3 2.5 %copy-start.10 = (pred[96]{0:T(512)(128)(4,1)S(1)}, pred[96]{0:T(512)(128)(4,1)}, u32[]{:S(2)}) copy-start(pred[96]{0:T(512)(128)(4,1)} %get-tuple-element.22) | copy-start | bytes 292
  106.3 3.7 %copy-start.7 = (f32[96,192]{1,0:T(8,128)}, f32[96,192]{1,0:T(8,128)S(1)}, u32[]{:S(2)}) copy-start(f32[96,192]{1,0:T(8,128)S(1)} %gather_fusion.8) | copy-start | bytes 221188
  116.9 1.7 %copy-start.11 = (pred[96]{0:T(512)(128)(4,1)S(1)}, pred[96]{0:T(512)(128)(4,1)}, u32[]{:S(2)}) copy-start(pred[96]{0:T(512)(128)(4,1)} %get-tuple-element.22) | copy-start | bytes 292
  116.9 1.7 %copy-start.17 = (f32[96]{0:T(128)S(1)}, f32[96]{0:T(128)}, u32[]{:S(2)}) copy-start(f32[96]{0:T(128)} %broadcast_add_fusion.1) | copy-start | bytes 1156
  118.6 2.5 %copy-start.13 = (s32[96]{0:T(128)S(1)}, s32[96]{0:T(128)}, u32[]{:S(2)}) copy-start(s32[96]{0:T(128)} %get-tuple-element.23) | copy-start | bytes 1156
  123.0 1.8 %copy-start.2 = (f32[96,2048]{1,0:T(8,128)S(1)}, f32[96,2048]{1,0:T(8,128)}, u32[]{:S(2)}) copy-start(f32[96,2048]{1,0:T(8,128)} %gather_fusion.15) | copy-start | bytes 2359300
  123.0 1.8 %copy-start.3 = (f32[96,2048]{1,0:T(8,128)S(1)}, f32[96,2048]{1,0:T(8,128)}, u32[]{:S(2)}) copy-start(f32[96,2048]{1,0:T(8,128)} %gather_fusion.12) | copy-start | bytes 2359300
  123.0 1.7 %copy-start.16 = (f32[96]{0:T(128)S(1)}, f32[96]{0:T(128)}, u32[]{:S(2)}) copy-start(f32[96]{0:T(128)} %broadcast_add_fusion) | copy-start | bytes 1156
  124.8 3.2 %copy-start.12 = (s32[96]{0:T(128)S(1)}, s32[96]{0:T(128)}, u32[]{:S(2)}) copy-start(s32[96]{0:T(128)} %get-tuple-element.24) | copy-start | bytes 1156
  (1 other events, 1.7 us)
